TPU v7x, 256 devices: a whole 4x4x8 slice. The times are simulated.
256 devices in a mesh: dp: 64 (over x, y, z_hi), tensor: 4 (over z_lo, core).
Axes of the slice: x: 4, y: 4, z: 8 (z_hi: 4, z_lo: 2; z = z_hi * 2 + z_lo), core: 2. Of those that a mesh axis runs over, the one named last changes fastest.
Arguments:
- tokens: bfloat16 [32768, 6144], P('dp', 'tensor'), may hold values from -6 to 6
- block_mask: int32 [128, 4, 4], P('dp'), may hold values from 0 to 1
- norm_gain: float32 [6144], replicated, may hold values from 0.25 to 1.75
- w_query: bfloat16 [6144, 3072], P('dp', 'tensor'), may hold values from -0.078125 to 0.078125
- w_key: bfloat16 [6144, 3072], P('dp', 'tensor'), may hold values from -0.078125 to 0.078125
- w_value: bfloat16 [6144, 3072], P('dp', 'tensor'), may hold values from -0.078125 to 0.078125
- query_gain: float32 [128], replicated, may hold values from 0.1 to 1.9
- key_gain: float32 [128], replicated, may hold values from 0.1 to 1.9
Outputs:
- attended: bfloat16 [32768, 3072], P('dp', 'tensor')
All inputs are finite; a program needn't handle non-finite values.
Results may differ from a plain program's by a relative error of at most 0.0085.
Values may be sent and summed in bfloat16 or wider, within the bound.
A program may use at most 192 MiB of HBM per device.

v0:
```python
import jax
import jax.numpy as jnp
from jax import lax
from jax.sharding import PartitionSpec as P

DH = 128
TPD = 256
BLOCK = 64
EPS = 1e-06


def sent_together(arrays, axis, dim, along):
    widths = [a.shape[along] for a in arrays]
    both = jnp.concatenate(arrays, axis=along)
    whole = lax.all_gather(both, axis, axis=dim, tiled=True)
    return tuple(jnp.split(whole, [sum(widths[:k]) for k in range(1, len(widths))], axis=along))


def layer_norm(rows, gain):
    values = rows.astype(jnp.float32)
    mean = jnp.mean(values, axis=-1, keepdims=True)
    mean_sq = jnp.mean(values * values, axis=-1, keepdims=True)
    return (values - mean) * lax.rsqrt(mean_sq - mean * mean + EPS) * gain


def head_norm(values, gain):
    mean_sq = jnp.mean(values * values, axis=-1, keepdims=True)
    return values * lax.rsqrt(mean_sq + EPS) * gain


def add_rows(normed, piece):
    return jnp.dot(normed, piece, preferred_element_type=jnp.float32)


def per_device(tokens, block_mask, norm_gain, w_query, w_key, w_value, query_gain, key_gain):
    whole = lax.all_gather(tokens, "tensor", axis=1, tiled=True)
    normed = layer_norm(whole, norm_gain).astype(jnp.bfloat16)
    pieces = sent_together((w_query, w_key, w_value), "dp", 0, 1)
    query = add_rows(normed, pieces[0])
    key = add_rows(normed, pieces[1])
    value = add_rows(normed, pieces[2])
    draws_here = tokens.shape[0] // TPD
    heads_here = w_query.shape[1] // DH
    query_n = head_norm(query.reshape(draws_here, TPD, heads_here, DH), query_gain).astype(
        jnp.bfloat16
    )
    key_n = head_norm(key.reshape(draws_here, TPD, heads_here, DH), key_gain).astype(jnp.bfloat16)
    value = value.astype(jnp.bfloat16).reshape(draws_here, TPD, heads_here, DH)
    blocks = block_mask.shape[-1]
    allowed = (block_mask > 0) | (jnp.arange(blocks)[:, None] == jnp.arange(blocks)[None, :])[None]
    allowed = jnp.repeat(jnp.repeat(allowed, BLOCK, axis=1), BLOCK, axis=2)
    scores = jnp.einsum(
        "bqhe,bkhe->bhqk", query_n, key_n, preferred_element_type=jnp.float32
    ) / jnp.sqrt(jnp.float32(DH))
    scores = jnp.where(allowed[:, None], scores, jnp.float32(-1e30))
    top = jnp.max(scores, axis=-1, keepdims=True)
    weights = jnp.exp(scores - top)
    probs = (weights / jnp.sum(weights, axis=-1, keepdims=True)).astype(jnp.bfloat16)
    out = jnp.einsum("bhqk,bkhe->bqhe", probs, value, preferred_element_type=jnp.float32)
    return out.astype(jnp.bfloat16).reshape(tokens.shape[0], heads_here * DH)


def solution(mesh):
    return jax.shard_map(
        per_device,
        mesh=mesh,
        in_specs=(
            P("dp", "tensor"),
            P("dp", None, None),
            P(),
            P("dp", "tensor"),
            P("dp", "tensor"),
            P("dp", "tensor"),
            P(),
            P(),
        ),
        out_specs=P("dp", "tensor"),
        check_vma=False,
    )
```

profile of v0, /device:TPU:6, one launch (start us, length us, event | category | flops | bytes accessed | tf_op | source)
XLA Modules:
  0.0 385.1 jit_solution(3754338296619104776)
XLA Ops:
  6.5 0.0 copy-start.3
  6.5 0.0 all-gather.3.cloned.1.call-start
  6.5 0.7 all-gather.3.cloned.1.call-update
  7.3 0.0 all-gather.5.cloned.1.call-start
  7.3 1.8 pad_maximum_fusion
  9.2 0.0 all-gather.5.cloned.1.call-update
  9.2 0.7 compare_or_fusion
  9.9 0.1 copy.15
  10.0 0.1 broadcast_in_dim.14
  10.1 0.1 reshape.68
  10.2 67.4 %all-gather.3.cloned.1.call-done = bf16[512,6144]{1,0:T(8,128)(2,1)} async-done(((bf16[512,1536]{1,0:T(8,128)(2,1)}), bf16[512,6144]{1,0:T(8,128)(2,1)}) %all-gather.3.cloned.1.call-update) | async-done | bytes 6291472 | tf_op jit(solution)/shard_map/all_gather | solution.py:36
  77.6 4.8 %convert_reduce_fusion = (f32[512]{0:T(512)S(1)}, f32[512]{0:T(512)S(1)}) fusion(bf16[512,6144]{1,0:T(8,128)(2,1)} %all-gather.3.cloned.1.call-done), kind=kLoop, calls=%fused_computation.3 | loop fusion | flops 12581888 | bytes 6295552 | tf_op jit(solution)/shard_map/reduce_sum | solution.py:21
  82.4 249.8 %all-gather.5.cloned.1.call-done = bf16[6144,2304]{1,0:T(8,128)(2,1)} async-done(((bf16[96,2304]{1,0:T(8,128)(2,1)}), bf16[6144,2304]{1,0:T(8,128)(2,1)}) %all-gather.5.cloned.1.call-update) | async-done | bytes 28311568 | tf_op jit(solution)/shard_map/all_gather | solution.py:15
  332.2 0.0 copy-done.3
  332.2 10.9 %fusion.17 = bf16[512,768]{1,0:T(8,128)(2,1)S(1)} fusion(bf16[6144,2304]{1,0:T(8,128)(2,1)} %all-gather.5.cloned.1.call-done, bf16[512,6144]{1,0:T(8,128)(2,1)} %all-gather.3.cloned.1.call-done, f32[6144]{0:T(1024)S(1)} %copy-done.3, f32[512]{0:T(512)S(1)} %get-tuple-element.8, f32[512]{0:T(512)S(1)} %get-tuple-element.7), kind=kOutput, calls=%fused_computation.27 | convolution fusion | flops 4847960064 | bytes 16543744 | tf_op jit(solution)/shard_map/dot_general | solution.py:32
  343.1 1.9 reshape.72
  345.0 10.9 %fusion.7 = f32[512,768]{0,1:T(8,128)S(1)} fusion(bf16[6144,2304]{1,0:T(8,128)(2,1)} %all-gather.5.cloned.1.call-done, bf16[512,6144]{1,0:T(8,128)(2,1)} %all-gather.3.cloned.1.call-done, f32[6144]{0:T(1024)S(1)} %copy-done.3, f32[512]{0:T(512)S(1)} %get-tuple-element.8, f32[512]{0:T(512)S(1)} %get-tuple-element.7), kind=kOutput, calls=%fused_computation.10 | convolution fusion | flops 4847566848 | bytes 17330176 | tf_op jit(solution)/shard_map/dot_general | solution.py:32
  355.9 1.0 reshape.69
  356.9 12.0 %fusion.5 = f32[512,768]{0,1:T(8,128)} fusion(bf16[6144,2304]{1,0:T(8,128)(2,1)} %all-gather.5.cloned.1.call-done, bf16[512,6144]{1,0:T(8,128)(2,1)} %all-gather.3.cloned.1.call-done, f32[6144]{0:T(1024)S(1)} %copy-done.3, f32[512]{0:T(512)S(1)} %get-tuple-element.8, f32[512]{0:T(512)S(1)} %get-tuple-element.7), kind=kOutput, calls=%fused_computation.8 | convolution fusion | flops 4847566848 | bytes 17330176 | tf_op jit(solution)/shard_map/dot_general | solution.py:32
  369.0 2.3 reshape.70
  371.3 0.6 multiply_reduce_fusion
  371.9 0.6 multiply_reduce_fusion.1
  372.5 0.0 copy-done.1
  372.6 0.0 copy-done.2
  372.6 1.6 multiply_convert_fusion
  374.2 0.0 copy-start
  374.2 0.6 fusion.22
  374.9 1.1 fusion.30
  376.0 0.0 copy-done
  376.0 0.5 fusion.20
  376.5 0.8 copy.29
  377.3 1.0 copy.39
  (7 shorter events, 0.1 us)
Async XLA Ops:
  6.5 325.7 %copy-start.3 = (f32[6144]{0:T(1024)S(1)}, f32[6144]{0:T(1024)}, u32[]{:S(2)}) copy-start(f32[6144]{0:T(1024)} %param.10) | copy-start | bytes 73732
  6.5 71.1 %all-gather.3.cloned.1.call-start = ((), (), s32[]{:S(2)}) async-start(), calls=%async_computation | async-start | bytes 7864320 | tf_op jit(solution)/shard_map/all_gather | solution.py:36
  7.3 325.0 %all-gather.5.cloned.1.call-start = ((), (), s32[]{:S(2)}) async-start(), calls=%async_computation.1 | async-start | bytes 28753920 | tf_op jit(solution)/shard_map/all_gather | solution.py:15
  369.0 3.6 copy-start.1
  369.0 3.6 copy-start.2
  374.2 1.8 copy-start
Sparse Core Ops, SparseCore 0:
  9.1 68.4 all-gather.2
  80.9 251.3 all-gather.4
where the time goes:
time: 385 us
  waiting for transfers between devices  318 us (83%)
  matrix products  34.9 us (9%)
  between operations  13.5 us (4%)
  other arithmetic  11.4 us (3%)
  local copies, waits for them, and re-layouts  7.26 us (2%)
    all_gather x1, waiting for transfers between devices, sent_together(): whole = lax.all_gather(both, axis, axis=dim, tiled=True)  250 us
    all_gather x1, waiting for transfers between devices, per_device(): whole = lax.all_gather(tokens, 'tensor', axis=1, tiled=True)  67.4 us
    dot_general x3, matrix products, add_rows(): return jnp.dot(normed, piece, preferred_element_type=jnp.float32)  33.8 us
  transfers between devices with their start and end apart: 2, of which 2 were waited for; matrix products, arithmetic and copies ran while one was open for 2% of the time, Pallas kernels for 0%

commit v1 on v0

--- a/solution.py
+++ b/solution.py
@@ -33,7 +33,9 @@
 
 
 def per_device(tokens, block_mask, norm_gain, w_query, w_key, w_value, query_gain, key_gain):
-    whole = lax.all_gather(tokens, "tensor", axis=1, tiled=True)
+    whole = jnp.concatenate(
+        lax.all_to_all(jnp.stack([tokens] * lax.axis_size("tensor")), "tensor", 0, 0), axis=1
+    )
     normed = layer_norm(whole, norm_gain).astype(jnp.bfloat16)
     pieces = sent_together((w_query, w_key, w_value), "dp", 0, 1)
     query = add_rows(normed, pieces[0])

time: 385 us -> 373 us (0.969)
  waiting for transfers between devices: 318 us -> 224 us
  local copies, waits for them, and re-layouts: 7.26 us -> 82.3 us
  matrix products: 34.9 us -> 26.1 us
  other arithmetic: 11.4 us -> 18.8 us
  starting transfers between devices: 0.04 us -> 5.37 us
    all_gather x1, waiting for transfers between devices: 250 us -> 61.4 us  [sent_together(): whole = lax.all_gather(both, axis, axis=dim, tiled=True)]
    all_to_all x0 -> x1, waiting for transfers between devices: none -> 163 us  [per_device(): lax.all_to_all(jnp.stack([tokens] * lax.axis_size('tensor')), 'tensor', 0...]
    all_gather x1 -> x0, waiting for transfers between devices: 67.4 us -> none  [per_device(): whole = lax.all_gather(tokens, 'tensor', axis=1, tiled=True)]
    dot_general x0 -> x3, local copies, waits for them, and re-layouts: none -> 40.1 us  [add_rows(): return jnp.dot(normed, piece, preferred_element_type=jnp.float32)]
    convert_element_type x0 -> x2, local copies, waits for them, and re-layouts: none -> 25.9 us  [per_device(): normed = layer_norm(whole, norm_gain).astype(jnp.bfloat16)]
    convert_element_type x1 -> x2, other arithmetic: 1.64 us -> 11.2 us  [per_device(): normed = layer_norm(whole, norm_gain).astype(jnp.bfloat16)]
    dot_general x3, matrix products: 33.8 us -> 24.9 us  [add_rows(): return jnp.dot(normed, piece, preferred_element_type=jnp.float32)]
    all_to_all x0 -> x1, local copies, waits for them, and re-layouts: none -> 8.71 us  [per_device(): lax.all_to_all(jnp.stack([tokens] * lax.axis_size('tensor')), 'tensor', 0...]
  transfers between devices with their start and end apart: 2 -> 2, of which waited for: 2 -> 2; matrix products, arithmetic and copies ran while one was open for 2% -> 15% of each run, Pallas kernels for 0% -> 0%
where the time goes in v1:
time: 373 us; the launch traced here: 370 us
  waiting for transfers between devices  224 us (60%)
  local copies, waits for them, and re-layouts  82.3 us (22%)
  matrix products  26.1 us (7%)
  other arithmetic  18.8 us (5%)
  between operations  13.6 us (4%)
  starting transfers between devices  5.37 us (1%)
    all_to_all x1, waiting for transfers between devices, per_device(): lax.all_to_all(jnp.stack([tokens] * lax.axis_size('tensor')), 'tensor', 0...  163 us
    all_gather x1, waiting for transfers between devices, sent_together(): whole = lax.all_gather(both, axis, axis=dim, tiled=True)  61.4 us
    dot_general x3, local copies, waits for them, and re-layouts, add_rows(): return jnp.dot(normed, piece, preferred_element_type=jnp.float32)  40.1 us
    convert_element_type x2, local copies, waits for them, and re-layouts, per_device(): normed = layer_norm(whole, norm_gain).astype(jnp.bfloat16)  25.9 us
    dot_general x3, matrix products, add_rows(): return jnp.dot(normed, piece, preferred_element_type=jnp.float32)  24.9 us
    convert_element_type x2, other arithmetic, per_device(): normed = layer_norm(whole, norm_gain).astype(jnp.bfloat16)  11.2 us
    all_to_all x1, local copies, waits for them, and re-layouts, per_device(): lax.all_to_all(jnp.stack([tokens] * lax.axis_size('tensor')), 'tensor', 0...  8.71 us
  transfers between devices with their start and end apart: 2, of which 2 were waited for; matrix products, arithmetic and copies ran while one was open for 15% of the time, Pallas kernels for 0%

profile of v1, /device:TPU:6, one launch (start us, length us, event | category | flops | bytes accessed | tf_op | source)
XLA Modules:
  0.0 370.3 jit_solution(10217594063985905002)
XLA Ops:
  6.5 1.8 pad_maximum_fusion
  8.4 0.0 all-gather.2.cloned.1.call-update
  8.4 4.5 %stack.2 = bf16[4,512,1536]{2,1,0:T(8,128)(2,1)} broadcast(bf16[512,1536]{1,0:T(8,128)(2,1)} %param.8), dimensions={1,2} | broadcast | bytes 7864320 | tf_op jit(solution)/shard_map/stack | solution.py:37
  12.9 5.4 %all-to-all-start = ((bf16[4,512,1536]{2,1,0:T(8,128)(2,1)}), bf16[4,512,1536]{2,1,0:T(8,128)(2,1)}, u32[]{:S(2)}, u32[]{:S(2)}) async-start(bf16[4,512,1536]{2,1,0:T(8,128)(2,1)} %stack.2), calls=%async_computation | async-start | bytes 12582912 | tf_op jit(solution)/shard_map/all_to_all | solution.py:37
  18.3 0.1 copy.38
  18.5 0.1 broadcast_in_dim.14
  18.5 0.1 reshape.131
  18.6 162.7 %all-to-all-done = bf16[4,512,1536]{2,1,0:T(8,128)(2,1)} async-done(((bf16[4,512,1536]{2,1,0:T(8,128)(2,1)}), bf16[4,512,1536]{2,1,0:T(8,128)(2,1)}, u32[]{:S(2)}, u32[]{:S(2)}) %all-to-all-start) | async-done | bytes 6291488 | tf_op jit(solution)/shard_map/all_to_all | solution.py:37
  181.4 8.7 %copy.36 = bf16[4,512,1536]{1,2,0:T(8,128)(2,1)} copy(bf16[4,512,1536]{2,1,0:T(8,128)(2,1)} %all-to-all-done) | data formatting | bytes 12582912 | tf_op jit(solution)/shard_map/all_to_all | solution.py:37
  190.1 4.6 %convert_reduce_fusion = (f32[512]{0:T(512)S(1)}, f32[512]{0:T(512)S(1)}) fusion(bf16[4,512,1536]{1,2,0:T(8,128)(2,1)} %copy.36), kind=kLoop, calls=%fused_computation.11 | loop fusion | flops 12581888 | bytes 6295552 | tf_op jit(solution)/shard_map/reduce_sum | solution.py:21
  194.7 4.0 %fusion.6 = bf16[512,4,1536]{0,2,1:T(8,128)(2,1)} fusion(bf16[4,512,1536]{1,2,0:T(8,128)(2,1)S(1)} %copy-done, f32[4,1536]{1,0:T(4,128)S(1)} %mul.109, f32[512]{0:T(512)S(1)} %get-tuple-element.10, f32[512]{0:T(512)S(1)} %get-tuple-element.9), kind=kLoop, calls=%fused_computation.12 | loop fusion | flops 15728640 | bytes 12611584 | tf_op jit(solution)/shard_map/convert_element_type | solution.py:39
  198.7 9.7 %reshape.138 = bf16[2,256,6144]{1,0,2:T(2,128)(2,1)} reshape(bf16[512,4,1536]{0,2,1:T(8,128)(2,1)} %fusion.6) | data formatting | bytes 12582912 | tf_op jit(solution)/shard_map/convert_element_type | solution.py:39
  208.4 16.2 %copy.48 = bf16[2,256,6144,1]{2,1,3,0:T(8,128)(2,1)} copy(bf16[2,256,6144,1]{1,0,2,3:T(2,128)(2,1)} %bitcast.40) | data formatting | bytes 12582912 | tf_op jit(solution)/shard_map/convert_element_type | solution.py:39
  224.6 7.2 %fusion.3 = bf16[512,6144]{0,1:T(8,128)(2,1)} fusion(bf16[4,512,1536]{1,2,0:T(8,128)(2,1)} %copy.36, f32[6144]{0:T(1024)S(1)} %copy-done.2, f32[512]{0:T(512)S(1)} %get-tuple-element.10, f32[512]{0:T(512)S(1)} %get-tuple-element.9), kind=kLoop, calls=%fused_computation.4 | loop fusion | flops 15728640 | bytes 12611584 | tf_op jit(solution)/shard_map/convert_element_type | solution.py:39
  231.8 61.4 %all-gather.2.cloned.1.call-done = bf16[6144,2304]{1,0:T(8,128)(2,1)} async-done(((bf16[96,2304]{1,0:T(8,128)(2,1)}), bf16[6144,2304]{1,0:T(8,128)(2,1)}) %all-gather.2.cloned.1.call-update) | async-done | bytes 28311568 | tf_op jit(solution)/shard_map/all_gather | solution.py:15
  293.2 14.6 %slice_bitcast_fusion = (bf16[768,6144]{0,1:T(8,128)(2,1)}, bf16[768,6144]{0,1:T(8,128)(2,1)}) fusion(bf16[6144,2304]{1,0:T(8,128)(2,1)} %all-gather.2.cloned.1.call-done), kind=kLoop, calls=%fused_computation.7 | loop fusion | bytes 37748736 | tf_op jit(solution)/shard_map/dot_general | solution.py:32
  307.9 12.7 %copy.41 = bf16[768,6144]{1,0:T(8,128)(2,1)} copy(bf16[768,6144]{0,1:T(8,128)(2,1)} %get-tuple-element.7) | data formatting | bytes 18874368 | tf_op jit(solution)/shard_map/dot_general | solution.py:32
  320.5 9.9 %fusion.13 = bf16[512,768]{1,0:T(8,128)(2,1)S(1)} fusion(bf16[512,6144]{0,1:T(8,128)(2,1)} %fusion.3, bf16[6144,2304]{1,0:T(8,128)(2,1)} %all-gather.2.cloned.1.call-done), kind=kOutput, calls=%fused_computation.26 | convolution fusion | flops 4832231424 | bytes 16515072 | tf_op jit(solution)/shard_map/dot_general | solution.py:32
  330.5 0.9 reshape.137
  331.3 0.0 slice-start
  331.4 12.8 %copy.40 = bf16[768,6144]{1,0:T(8,128)(2,1)} copy(bf16[768,6144]{0,1:T(8,128)(2,1)} %get-tuple-element.8) | data formatting | bytes 18874368 | tf_op jit(solution)/shard_map/dot_general | solution.py:32
  344.2 9.9 %multiply_reduce_fusion.1 = (f32[2,256,6]{1,2,0:T(8,128)S(1)}, f32[2,256,6,128]{1,3,2,0:T(8,128)S(1)}) fusion(bf16[2,256,6144,1]{2,1,3,0:T(8,128)(2,1)} %copy.48, bf16[6,128,6144,1]{2,1,0,3:T(8,128)(2,1)} %bitcast.41), kind=kOutput, calls=%fused_computation.20 | convolution fusion | flops 4832621568 | bytes 17313792 | tf_op jit(solution)/shard_map/dot_general | solution.py:32
  354.1 0.0 slice-done
  354.1 0.0 copy-done.1
  354.1 0.0 copy-start.4
  354.1 0.0 copy-start.5
  354.1 5.1 %multiply_reduce_fusion.2 = (f32[2,256,6]{1,2,0:T(8,128)S(1)}, f32[2,256,6,128]{1,3,2,0:T(8,128)S(1)}) fusion(bf16[2,256,6144,1]{2,1,3,0:T(8,128)(2,1)S(1)} %bitcast.44, bf16[6,128,6144,1]{2,1,0,3:T(8,128)(2,1)S(1)} %bitcast.42), kind=kOutput, calls=%fused_computation.22 | convolution fusion | flops 4832621568 | bytes 17313792 | tf_op jit(solution)/shard_map/dot_general | solution.py:32
  359.3 0.7 fusion.17
  360.1 1.1 fusion.25
  361.2 0.5 fusion.16
  361.7 0.8 copy.57
  362.4 1.0 copy.63
  (19 shorter events, 0.1 us)
Async XLA Ops:
  6.5 286.7 %all-gather.2.cloned.1.call-start = ((), (), s32[]{:S(2)}) async-start(), calls=%async_computation.1 | async-start | bytes 28753920 | tf_op jit(solution)/shard_map/all_gather | solution.py:15
  12.9 5.4 %copy-start.3 = (s32[2,4,4]{2,1,0:T(4,128)S(1)}, s32[2,4,4]{2,1,0:T(4,128)}, u32[]{:S(2)}) copy-start(s32[2,4,4]{2,1,0:T(4,128)} %param.9) | copy-start | bytes 388
  12.9 5.7 %copy-start.2 = (f32[6144]{0:T(1024)S(1)}, f32[6144]{0:T(1024)}, u32[]{:S(2)}) copy-start(f32[6144]{0:T(1024)} %param.10) | copy-start | bytes 73732
  12.9 168.4 %all-to-all-start = ((bf16[4,512,1536]{2,1,0:T(8,128)(2,1)}), bf16[4,512,1536]{2,1,0:T(8,128)(2,1)}, u32[]{:S(2)}, u32[]{:S(2)}) async-start(bf16[4,512,1536]{2,1,0:T(8,128)(2,1)} %stack.2), calls=%async_computation | async-start | bytes 12582912 | tf_op jit(solution)/shard_map/all_to_all | solution.py:37
  190.1 4.6 %copy-start = (bf16[4,512,1536]{1,2,0:T(8,128)(2,1)S(1)}, bf16[4,512,1536]{1,2,0:T(8,128)(2,1)}, u32[]{:S(2)}) copy-start(bf16[4,512,1536]{1,2,0:T(8,128)(2,1)} %copy.36) | copy-start | bytes 18874372
  331.3 22.7 %slice-start = ((s8[6291456]{0:T(1024)(128)(4,1)}), s8[2097152]{0:T(1024)(128)(4,1)S(1)}, s32[]{:S(2)}) async-start(s8[6291456]{0:T(1024)(128)(4,1)} %bitcast.43), calls=%async_computation.2 | async-start | bytes 4194304
  344.2 9.9 %copy-start.1 = (bf16[768,6144]{1,0:T(8,128)(2,1)S(1)}, bf16[768,6144]{1,0:T(8,128)(2,1)}, u32[]{:S(2)}) copy-start(bf16[768,6144]{1,0:T(8,128)(2,1)} %copy.40) | copy-start | bytes 28311556
  344.2 9.9 %slice-start.1 = ((s8[6291456]{0:T(1024)(128)(4,1)}), s8[4194304]{0:T(1024)(128)(4,1)S(1)}, s32[]{:S(2)}) async-start(s8[6291456]{0:T(1024)(128)(4,1)} %bitcast.43), calls=%async_computation.3 | async-start | bytes 8388608
  354.1 5.1 %copy-start.4 = (f32[128]{0:T(128)S(1)}, f32[128]{0:T(128)}, u32[]{:S(2)}) copy-start(f32[128]{0:T(128)} %param.15) | copy-start | bytes 1540
  354.1 5.1 %copy-start.5 = (f32[128]{0:T(128)S(1)}, f32[128]{0:T(128)}, u32[]{:S(2)}) copy-start(f32[128]{0:T(128)} %param.14) | copy-start | bytes 1540
Sparse Core Ops, SparseCore 0:
  10.6 282.5 all-gather.1
